TPU v7x, 32 devices: a whole 2x2x4 slice. The times are simulated.
32 devices in a mesh: dp: 8 (over z, x), fsdp: 4 (over y, core).
Axes of the slice: x: 2, y: 2, z: 4, core: 2. Of those that a mesh axis runs over, the one named last changes fastest.
Arguments:
- tokens: bfloat16 [32, 169, 1024], P(('dp', 'fsdp')), may hold values from -6 to 6
- out_grad: bfloat16 [32, 169, 1024], P(('dp', 'fsdp')), may hold values from -6 to 6
- text_len: int32 [32], P(('dp', 'fsdp')), may hold values from 12 to 120
- x_bucket: int32 [32, 169], P(('dp', 'fsdp')), may hold values from 0 to 127
- y_bucket: int32 [32, 169], P(('dp', 'fsdp')), may hold values from 0 to 127
- patch_mask: int32 [32, 49], P(('dp', 'fsdp')), may hold values 0 or 1
- qkv_weight: bfloat16 [1024, 3072], P(('dp', 'fsdp')), may hold values from -0.1875 to 0.1875
- qv_bias: bfloat16 [2048], P(('dp', 'fsdp')), may hold values from -3 to 3
- proj_weight: bfloat16 [1024, 1024], P(('dp', 'fsdp')), may hold values from -1 to 1
- proj_bias: bfloat16 [1024], P(('dp', 'fsdp')), may hold values from -2 to 2
- first_gain: bfloat16 [1024], P(('dp', 'fsdp')), may hold values from 0.5 to 1.5
- first_shift: bfloat16 [1024], P(('dp', 'fsdp')), may hold values from -2 to 2
- rel_tables: bfloat16 [6144], P(('dp', 'fsdp')), may hold values from -4 to 4
- up_weight: bfloat16 [1024, 4096], P(('dp', 'fsdp')), may hold values from -0.1875 to 0.1875
- up_bias: bfloat16 [4096], P(('dp', 'fsdp')), may hold values from -3 to 3
- down_weight: bfloat16 [1024, 4096], P(('dp', 'fsdp')), may hold values from -0.09375 to 0.09375
- down_bias: bfloat16 [1024], P(('dp', 'fsdp')), may hold values from -2 to 2
- second_gain: bfloat16 [1024], P(('dp', 'fsdp')), may hold values from 0.5 to 1.5
- second_shift: bfloat16 [1024], P(('dp', 'fsdp')), may hold values from -2 to 2
Outputs:
- encoded: bfloat16 [32, 169, 1024], P(('dp', 'fsdp'))
- grad_tokens: float32 [32, 169, 1024], P(('dp', 'fsdp'))
- grad_qkv: float32 [1024, 3072], P(('dp', 'fsdp'))
- grad_qvbias: float32 [2048], P(('dp', 'fsdp'))
- grad_proj: float32 [1024, 1024], P(('dp', 'fsdp'))
- grad_projbias: float32 [1024], P(('dp', 'fsdp'))
- grad_firstgain: float32 [1024], P(('dp', 'fsdp'))
- grad_firstshift: float32 [1024], P(('dp', 'fsdp'))
- grad_tables: float32 [6144], P(('dp', 'fsdp'))
- grad_up: float32 [1024, 4096], P(('dp', 'fsdp'))
- grad_upbias: float32 [4096], P(('dp', 'fsdp'))
- grad_down: float32 [1024, 4096], P(('dp', 'fsdp'))
- grad_downbias: float32 [1024], P(('dp', 'fsdp'))
- grad_secondgain: float32 [1024], P(('dp', 'fsdp'))
- grad_secondshift: float32 [1024], P(('dp', 'fsdp'))
All inputs are finite; a program needn't handle non-finite values. No bound on the sum of `patch_mask` on one device may be relied on, other than what follows from the above.
Results may differ from a plain program's by a relative error of at most 0.015.
Values may be sent and summed in bfloat16 or wider, within the bound.
No kernel may reach another device: no remote copies, remote signals or barrier semaphores. Data moves between devices by JAX's collectives and lax.ppermute only.
A program may use at most 256 MiB of HBM per device.

v0:
```python
from functools import partial
import jax
import jax.numpy as jnp
from jax import lax
from jax.sharding import PartitionSpec as P

D = 1024
H = 16
HD = 64
FF = 4096
NB = 128
TEXT = 120
SLOTS = 169
HIGHEST = lax.Precision.HIGHEST
NEGATIVE = -1e30
EPSILON = 1e-05


def layer_norm(values, norm_gain, norm_shift):
    average = jnp.mean(values, axis=-1, keepdims=True)
    centred = values - average
    spread = jnp.mean(centred * centred, axis=-1, keepdims=True)
    return centred * lax.rsqrt(spread + EPSILON) * norm_gain + norm_shift


def key_valid(text_len, patch_mask):
    places = jnp.arange(TEXT, dtype=jnp.int32)
    text_part = places[None, :] < text_len[:, None]
    return jnp.concatenate([text_part, patch_mask > 0], axis=1)


def relative_table(buckets):
    indices = jnp.arange(buckets, dtype=jnp.int32)
    offsets = (
        jnp.clip(indices[None, :] - indices[:, None], -(buckets // 2), buckets // 2 - 1)
        + buckets // 2
    )
    return offsets[:, :, None] == indices[None, None, :]


def right_product(left, right):
    return lax.dot_general(
        left, right, (((1,), (1,)), ((), ())), preferred_element_type=jnp.float32
    )


def rows_product(left, right):
    return lax.dot_general(
        left, right, (((0,), (0,)), ((), ())), preferred_element_type=jnp.float32
    )


def local(
    tokens,
    out_grad,
    text_len,
    x_bucket,
    y_bucket,
    patch_mask,
    qkv_weight,
    qv_bias,
    proj_weight,
    proj_bias,
    first_gain,
    first_shift,
    rel_tables,
    up_weight,
    up_bias,
    down_weight,
    down_bias,
    second_gain,
    second_shift,
):
    f32 = jnp.float32
    bf16 = jnp.bfloat16
    qkv_full, proj_full, qv_full, projb_full, gain_one, shift_one, tables_full = (
        lax.all_gather(qkv_weight, ("dp", "fsdp"), axis=0, tiled=True),
        lax.all_gather(proj_weight, ("dp", "fsdp"), axis=0, tiled=True),
        lax.all_gather(qv_bias, ("dp", "fsdp"), axis=0, tiled=True),
        lax.all_gather(proj_bias, ("dp", "fsdp"), axis=0, tiled=True),
        lax.all_gather(first_gain, ("dp", "fsdp"), axis=0, tiled=True),
        lax.all_gather(first_shift, ("dp", "fsdp"), axis=0, tiled=True),
        lax.all_gather(rel_tables, ("dp", "fsdp"), axis=0, tiled=True),
    )
    up_full, down_full, upb_full, downb_full, gain_two, shift_two = (
        lax.all_gather(up_weight, ("dp", "fsdp"), axis=0, tiled=True),
        lax.all_gather(down_weight, ("dp", "fsdp"), axis=0, tiled=True),
        lax.all_gather(up_bias, ("dp", "fsdp"), axis=0, tiled=True),
        lax.all_gather(down_bias, ("dp", "fsdp"), axis=0, tiled=True),
        lax.all_gather(second_gain, ("dp", "fsdp"), axis=0, tiled=True),
        lax.all_gather(second_shift, ("dp", "fsdp"), axis=0, tiled=True),
    )
    doc_count = tokens.shape[0]
    row_total = doc_count * SLOTS
    valid_keys = key_valid(text_len, patch_mask)
    row_keep = valid_keys.reshape(row_total, 1).astype(f32)
    key_mask = valid_keys[:, None, :]
    positions = jnp.arange(SLOTS, dtype=jnp.int32) * NB // SLOTS
    position_ids = positions[None, :]
    all_ids = jnp.stack([position_ids, x_bucket, y_bucket], axis=2)
    buckets = jnp.arange(NB, dtype=jnp.int32)
    one_hot = (all_ids[..., None] == buckets).astype(bf16)
    key_codes = one_hot.reshape(doc_count, SLOTS, 3 * NB)
    relation = relative_table(NB)
    table_grid = tables_full.reshape(3, H, NB)
    toeplitz = jnp.einsum(
        "khr,abr->khab", table_grid, relation.astype(bf16), preferred_element_type=f32
    ).astype(bf16)
    query_codes = (
        jnp.einsum("dika,khab->hdikb", one_hot, toeplitz, preferred_element_type=f32)
        .astype(bf16)
        .reshape(H, doc_count, SLOTS, 3 * NB)
    )
    rows_in = tokens.reshape(row_total, D)
    qkv_bias = jnp.concatenate(
        [qv_full[:D].astype(f32), jnp.zeros((D,), f32), qv_full[D:].astype(f32)]
    )
    qkv_rows = (jnp.dot(rows_in, qkv_full, preferred_element_type=f32) + qkv_bias).astype(bf16)
    head_major = qkv_rows.reshape(doc_count, SLOTS, 3, H, HD).transpose(2, 3, 0, 1, 4)
    queries = head_major[0]
    keys_all = head_major[1]
    values_all = head_major[2]

    def scores_for(query_h, key_h, code_h):
        content = jnp.einsum("die,dje->dij", query_h, key_h, preferred_element_type=f32) * 0.125
        spatial = jnp.einsum("dic,djc->dij", code_h, key_codes, preferred_element_type=f32)
        return jnp.where(key_mask, content + spatial, NEGATIVE)

    def attend(inputs):
        query_h, key_h, value_h, code_h = inputs
        scores = scores_for(query_h, key_h, code_h)
        row_peak = jnp.max(scores, axis=-1, keepdims=True)
        exponent = jnp.exp(scores - row_peak)
        row_sum = jnp.sum(exponent, axis=-1, keepdims=True)
        probs_low = (exponent / row_sum).astype(bf16)
        mixed_h = jnp.einsum("dij,dje->die", probs_low, value_h, preferred_element_type=f32).astype(
            bf16
        )
        return (mixed_h, (row_peak + jnp.log(row_sum))[..., 0])

    head_out, log_norm = lax.map(attend, (queries, keys_all, values_all, query_codes))
    attended = head_out.transpose(1, 2, 0, 3).reshape(row_total, D)
    branch = jnp.dot(attended, proj_full, preferred_element_type=f32) + projb_full.astype(f32)
    resid_one = rows_in.astype(f32) + branch
    gain_onef = gain_one.astype(f32)
    shift_onef = shift_one.astype(f32)
    normed_one = layer_norm(resid_one, gain_onef, shift_onef)
    normed_low = normed_one.astype(bf16)
    pre_act = jnp.dot(normed_low, up_full, preferred_element_type=f32) + upb_full.astype(f32)
    act_low = jax.nn.gelu(pre_act, approximate=False).astype(bf16)
    ffn_out = right_product(act_low, down_full) + downb_full.astype(f32)
    resid_two = normed_one + ffn_out
    gain_twof = gain_two.astype(f32)
    shift_twof = shift_two.astype(f32)
    final_rows = layer_norm(resid_two, gain_twof, shift_twof) * row_keep
    encoded = final_rows.astype(bf16).reshape(doc_count, SLOTS, D)
    qkv_back, proj_back = (
        lax.all_gather(qkv_weight, ("dp", "fsdp"), axis=0, tiled=True),
        lax.all_gather(proj_weight, ("dp", "fsdp"), axis=0, tiled=True),
    )
    up_back, down_back = (
        lax.all_gather(up_weight, ("dp", "fsdp"), axis=0, tiled=True),
        lax.all_gather(down_weight, ("dp", "fsdp"), axis=0, tiled=True),
    )
    grad_rows = out_grad.reshape(row_total, D).astype(f32) * row_keep
    unused, norm_two_back = jax.vjp(layer_norm, resid_two, gain_twof, shift_twof)
    d_resid_two, d_gain_two, d_shift_two = norm_two_back(grad_rows)
    d_ffn = d_resid_two.astype(bf16)
    d_down_bias = jnp.sum(d_ffn, axis=0, dtype=f32)
    d_act = jnp.dot(d_ffn, down_back, preferred_element_type=f32)
    unused, gelu_back = jax.vjp(partial(jax.nn.gelu, approximate=False), pre_act)
    d_pre = gelu_back(d_act)[0].astype(bf16)
    d_up_bias = jnp.sum(d_pre, axis=0, dtype=f32)
    d_normed = d_resid_two + right_product(d_pre, up_back)
    unused, norm_one_back = jax.vjp(layer_norm, resid_one, gain_onef, shift_onef)
    d_resid_one, d_gain_one, d_shift_one = norm_one_back(d_normed)
    d_branch = d_resid_one.astype(bf16)
    d_proj_bias = jnp.sum(d_branch, axis=0, dtype=f32)
    d_attended = right_product(d_branch, proj_back).astype(bf16)
    d_heads = d_attended.reshape(doc_count, SLOTS, H, HD).transpose(2, 0, 1, 3)
    hot_float = one_hot.astype(f32)

    def attend_back(inputs):
        query_h, key_h, value_h, code_h, d_out_h, log_h = inputs
        scores = scores_for(query_h, key_h, code_h)
        probability = jnp.exp(scores - log_h[..., None])
        d_probs = jnp.einsum("die,dje->dij", d_out_h, value_h, preferred_element_type=f32)
        d_scores = (
            probability * (d_probs - jnp.sum(probability * d_probs, axis=-1, keepdims=True))
        ).astype(bf16)
        probs_low = probability.astype(bf16)
        d_value = jnp.einsum("dij,die->dje", probs_low, d_out_h, preferred_element_type=f32)
        d_query = jnp.einsum("dij,dje->die", d_scores, key_h, preferred_element_type=f32) * 0.125
        d_key = jnp.einsum("dij,die->dje", d_scores, query_h, preferred_element_type=f32) * 0.125
        d_codes = jnp.einsum(
            "dij,djc->dic", d_scores, key_codes, preferred_element_type=f32
        ).reshape(doc_count, SLOTS, 3, NB)
        d_grid = jnp.einsum("dika,dikb->kab", hot_float, d_codes, precision=HIGHEST)
        return ((d_query.astype(bf16), d_key.astype(bf16), d_value.astype(bf16)), d_grid)

    (d_query_all, d_key_all, d_value_all), d_grids = lax.map(
        attend_back, (queries, keys_all, values_all, query_codes, d_heads, log_norm)
    )
    d_qkv = (
        jnp.stack([d_query_all, d_key_all, d_value_all])
        .transpose(2, 3, 0, 1, 4)
        .reshape(row_total, 3 * D)
    )
    d_qv_bias = jnp.concatenate(
        [jnp.sum(d_qkv[:, :D], axis=0, dtype=f32), jnp.sum(d_qkv[:, 2 * D :], axis=0, dtype=f32)]
    )
    grad_tokens = d_resid_one + right_product(d_qkv, qkv_back)
    d_tables = jnp.einsum(
        "hkab,abr->khr", d_grids, relation.astype(f32), precision=HIGHEST
    ).reshape(3 * H * NB)
    outer_count = lax.axis_size("dp")
    inner_count = lax.axis_size("fsdp")
    block_rows = D // (outer_count * inner_count)
    columns = 4 * D + 2 * FF
    term = jnp.concatenate(
        [
            rows_product(rows_in, d_qkv),
            rows_product(attended, d_branch),
            rows_product(normed_low, d_pre),
            rows_product(d_ffn, act_low),
        ],
        axis=1,
    )
    arrived = lax.all_to_all(
        term.reshape(outer_count, D // outer_count, columns).astype(jnp.bfloat16),
        "dp",
        split_axis=0,
        concat_axis=0,
        tiled=True,
    ).astype(jnp.float32)
    outer_rows = jnp.sum(arrived, axis=0)
    arrived_inner = lax.all_to_all(
        outer_rows.reshape(inner_count, block_rows, columns).astype(jnp.bfloat16),
        "fsdp",
        split_axis=0,
        concat_axis=0,
        tiled=True,
    ).astype(jnp.float32)
    weight_rows = jnp.sum(arrived_inner, axis=0)
    grad_qkv = weight_rows[:, : 3 * D]
    grad_proj = weight_rows[:, 3 * D : 4 * D]
    grad_up = weight_rows[:, 4 * D : 4 * D + FF]
    grad_down = weight_rows[:, 4 * D + FF :]
    (
        grad_qvbias,
        grad_projbias,
        grad_firstgain,
        grad_firstshift,
        grad_tables,
        grad_upbias,
        grad_downbias,
        grad_secondgain,
        grad_secondshift,
    ) = (
        lax.psum_scatter(d_qv_bias, ("dp", "fsdp"), scatter_dimension=0, tiled=True),
        lax.psum_scatter(d_proj_bias, ("dp", "fsdp"), scatter_dimension=0, tiled=True),
        lax.psum_scatter(d_gain_one, ("dp", "fsdp"), scatter_dimension=0, tiled=True),
        lax.psum_scatter(d_shift_one, ("dp", "fsdp"), scatter_dimension=0, tiled=True),
        lax.psum_scatter(d_tables, ("dp", "fsdp"), scatter_dimension=0, tiled=True),
        lax.psum_scatter(d_up_bias, ("dp", "fsdp"), scatter_dimension=0, tiled=True),
        lax.psum_scatter(d_down_bias, ("dp", "fsdp"), scatter_dimension=0, tiled=True),
        lax.psum_scatter(d_gain_two, ("dp", "fsdp"), scatter_dimension=0, tiled=True),
        lax.psum_scatter(d_shift_two, ("dp", "fsdp"), scatter_dimension=0, tiled=True),
    )
    return (
        encoded,
        grad_tokens.reshape(doc_count, SLOTS, D),
        grad_qkv,
        grad_qvbias,
        grad_proj,
        grad_projbias,
        grad_firstgain,
        grad_firstshift,
        grad_tables,
        grad_up,
        grad_upbias,
        grad_down,
        grad_downbias,
        grad_secondgain,
        grad_secondshift,
    )


def solution(mesh):
    return jax.shard_map(
        local,
        mesh=mesh,
        in_specs=(
            P(("dp", "fsdp"), None, None),
            P(("dp", "fsdp"), None, None),
            P(("dp", "fsdp")),
            P(("dp", "fsdp"), None),
            P(("dp", "fsdp"), None),
            P(("dp", "fsdp"), None),
            P(("dp", "fsdp"), None),
            P(("dp", "fsdp")),
            P(("dp", "fsdp"), None),
            P(("dp", "fsdp")),
            P(("dp", "fsdp")),
            P(("dp", "fsdp")),
            P(("dp", "fsdp")),
            P(("dp", "fsdp"), None),
            P(("dp", "fsdp")),
            P(("dp", "fsdp"), None),
            P(("dp", "fsdp")),
            P(("dp", "fsdp")),
            P(("dp", "fsdp")),
        ),
        out_specs=(
            P(("dp", "fsdp"), None, None),
            P(("dp", "fsdp"), None, None),
            P(("dp", "fsdp"), None),
            P(("dp", "fsdp")),
            P(("dp", "fsdp"), None),
            P(("dp", "fsdp")),
            P(("dp", "fsdp")),
            P(("dp", "fsdp")),
            P(("dp", "fsdp")),
            P(("dp", "fsdp"), None),
            P(("dp", "fsdp")),
            P(("dp", "fsdp"), None),
            P(("dp", "fsdp")),
            P(("dp", "fsdp")),
            P(("dp", "fsdp")),
        ),
        check_vma=False,
    )
```

profile of v0, /device:TPU:8, one launch (start us, length us, event | category | flops | bytes accessed | tf_op | source)
XLA Modules:
  0.0 1361.8 jit_solution(18023036616747059392)
XLA Ops:
  18.1 41.5 %all-reduce.18 = (bf16[2048]{0:T(1024)(128)(2,1)S(1)}, bf16[6144]{0:T(1024)(128)(2,1)S(1)}, bf16[1024]{0:T(1024)(128)(2,1)S(1)}, bf16[1024]{0:T(1024)(128)(2,1)S...) all-reduce(bf16[2048]{0:T(1024)(128)(2,1)S(1)} %dynamic-update-slic, ...), channel_id=1, replica_groups=mesh['dp'=8,'fsdp'=4] {'dp','fsdp'}, use_global_device_ids=true, to_apply=%add | all-reduce | flops 14336 | bytes 57344
  59.7 34.3 %all-gather = bf16[32,1,128]{2,1,0:T(2,128)(2,1)S(1)} all-gather(bf16[1,1,128]{2,1,0:T(2,128)(2,1)} %bitcast.272), channel_id=1, replica_groups=mesh['dp'=8,'fsdp'=4] {'dp','fsdp'}, dimensions={0}, use_global_device_ids=true | all-gather | bytes 8448 | tf_op jit(solution)/shard_map/all_gather | solution.py:88
  120.6 45.8 %while.31 = (s32[]{:T(128)}, bf16[16,1,169,64]{2,3,1,0:T(8,128)(2,1)S(1)}, f32[16,1,169]{2,1,0:T(1,128)S(1)}, pred[1,1,169]{2,1,0:T(4,128)(4,1)S(1)}, bf16[16,1,...) while((s32[]{:T(128)}, ...), condition=%wide.region_3.4_spmd.clone, body=%wide.region_0.3_spmd.clone.sunk | while | flops 29643952 | bytes 1993045 | solution.py:141
  169.8 49.5 %all-gather.10.cloned.1.call-done = bf16[1024,4096]{1,0:T(8,128)(2,1)} async-done(((bf16[32,4096]{1,0:T(8,128)(2,1)}), bf16[1024,4096]{1,0:T(8,128)(2,1)}) %all-gather.10.cloned.1.call-update) | async-done | bytes 8388624 | tf_op jit(solution)/shard_map/all_gather | solution.py:86
  219.3 12.2 multiply_convert_fusion.1
  231.6 66.6 %all-gather.12.cloned.1.call-done = bf16[1024,4096]{1,0:T(8,128)(2,1)} async-done(((bf16[32,4096]{1,0:T(8,128)(2,1)}), bf16[1024,4096]{1,0:T(8,128)(2,1)}) %all-gather.12.cloned.1.call-update) | async-done | bytes 8388624 | tf_op jit(solution)/shard_map/all_gather | solution.py:87
  298.2 7.0 fusion.122
  308.4 5.6 convolution_convert_fusion.2
  319.2 5.7 convolution_convert_fusion.3
  335.2 262.0 %while.32 = (s32[]{:T(128)}, bf16[16,1,169,64]{2,3,1,0:T(8,128)(2,1)}, bf16[16,1,169,64]{2,3,1,0:T(8,128)(2,1)}, bf16[16,1,169,64]{2,3,1,0:T(8,128)(2,1)}, f32[1...) while((s32[]{:T(128)}, ...), condition=%wide.region_14.15_spmd.clone.clone, body=%wide.region_12.14_spmd.clone.clone.sunk | while | flops 162622784 | bytes 5006393 | solution.py:201
  345.1 6.5 dynamic_update_slice.47
  361.4 6.5 dynamic_update_slice.47
  377.8 6.5 dynamic_update_slice.47
  394.2 6.5 dynamic_update_slice.47
  410.5 6.5 dynamic_update_slice.47
  426.9 6.5 dynamic_update_slice.47
  443.2 6.5 dynamic_update_slice.47
  459.6 6.5 dynamic_update_slice.47
  475.9 6.5 dynamic_update_slice.47
  492.3 6.5 dynamic_update_slice.47
  508.7 6.5 dynamic_update_slice.47
  525.1 6.5 dynamic_update_slice.47
  541.5 6.5 dynamic_update_slice.47
  557.9 6.5 dynamic_update_slice.47
  574.3 6.5 dynamic_update_slice.47
  590.7 6.5 dynamic_update_slice.47
  606.0 8.7 copy.122
  614.7 17.5 %pad_maximum_fusion = bf16[1024,12288]{1,0:T(8,128)(2,1)} fusion(bf16[1024,4096]{1,0:T(8,128)(2,1)} %convolution_convert_fusion.2, bf16[1024,4096]{1,0:T(8,128)(2,1)} %convolution_convert_fusion.3, bf16[1024,1024]{1,0:T(8,128)(2,1)} %copy.123, bf16[1024,3072]{1,0:T(8,128)(2,1)} %copy.122), kind=kLoop, calls=%fused_computation.85 | loop fusion | flops 100663296 | bytes 50331648 | tf_op jit(solution)/shard_map/concatenate | solution.py:220
  632.2 552.2 %all_to_all.10 = bf16[8,128,12288]{2,1,0:T(8,128)(2,1)} all-to-all(bf16[8,128,12288]{2,1,0:T(8,128)(2,1)} %bitcast.252), channel_id=1, replica_groups=mesh['dp'=8,'fsdp'=4] {'dp'}, dimensions={0} | all-to-all | bytes 50331648 | tf_op jit(solution)/shard_map/all_to_all | solution.py:229
  1184.5 15.2 %reduce_sum.205 = bf16[128,12288]{1,0:T(8,128)(2,1)} reduce(bf16[8,128,12288]{2,1,0:T(8,128)(2,1)} %all_to_all.10, bf16[]{:T(256)} %constant.70.clone.1), dimensions={0}, to_apply=%region_15.16 | reduce | flops 11010048 | bytes 28311554 | tf_op jit(solution)/shard_map/reduce_sum | solution.py:236
  1205.6 6.0 fusion.73
  1218.3 120.3 %all-reduce.21.cloned.1.call-done = (f32[2048]{0:T(1024)}, f32[1024]{0:T(1024)}, f32[1024]{0:T(1024)}, f32[1024]{0:T(1024)}, f32[6144]{0:T(1024)}, /*index=5*/f3...) async-done(((f32[2048]{0:T(1024)}, f32[1024]{0:T(1024)}, f32[1024]{0:T(1024)}, f32[1024]{0:T(1024)}, f32[6144]{0:T(1024)}, /*index=5*/f32[4096]{0:T(1024)}, ...) | async-done | bytes 73744
  (555 shorter events, 298.2 us)
Async XLA Ops:
  7.2 101.6 %all-gather.6.cloned.1.call-start = ((), (), s32[]{:S(2)}) async-start(), calls=%async_computation.2 | async-start | bytes 6488064 | tf_op jit(solution)/shard_map/all_gather | solution.py:77
  7.9 158.6 %all-gather.8.cloned.1.call-start = ((), (), s32[]{:S(2)}) async-start(), calls=%async_computation.3 | async-start | bytes 2162688 | tf_op jit(solution)/shard_map/all_gather | solution.py:78
  8.7 210.6 %all-gather.10.cloned.1.call-start = ((), (), s32[]{:S(2)}) async-start(), calls=%async_computation.4 | async-start | bytes 8650752 | tf_op jit(solution)/shard_map/all_gather | solution.py:86
  9.4 288.8 %all-gather.12.cloned.1.call-start = ((), (), s32[]{:S(2)}) async-start(), calls=%async_computation.5 | async-start | bytes 8650752 | tf_op jit(solution)/shard_map/all_gather | solution.py:87
  103.1 5.7 copy-start.7
  166.5 65.1 %copy-start.3 = (bf16[16,1,169,64]{2,3,1,0:T(8,128)(2,1)}, bf16[16,1,169,64]{2,3,1,0:T(8,128)(2,1)S(1)}, u32[]{:S(2)}) copy-start(bf16[16,1,169,64]{2,3,1,0:T(8,128)(2,1)S(1)} %get-tuple-element.138) | copy-start | bytes 1038340
  166.5 65.1 %copy-start.5 = (bf16[16,1,169,64]{3,2,1,0:T(8,128)(2,1)}, bf16[16,1,169,64]{3,2,1,0:T(8,128)(2,1)S(1)}, u32[]{:S(2)}) copy-start(bf16[16,1,169,64]{3,2,1,0:T(8,128)(2,1)S(1)} %get-tuple-element.782) | copy-start | bytes 1038340
  166.5 65.1 %copy-start.6 = (bf16[16,1,169,64]{3,2,1,0:T(8,128)(2,1)}, bf16[16,1,169,64]{3,2,1,0:T(8,128)(2,1)S(1)}, u32[]{:S(2)}) copy-start(bf16[16,1,169,64]{3,2,1,0:T(8,128)(2,1)S(1)} %get-tuple-element.783) | copy-start | bytes 1038340
  298.2 7.3 copy-start.9
  298.2 15.8 %slice-start.2 = ((s8[8388608]{0:T(1024)(128)(4,1)}), s8[4194304]{0:T(1024)(128)(4,1)S(1)}, s32[]{:S(2)}) async-start(s8[8388608]{0:T(1024)(128)(4,1)} %bitcast.275), calls=%async_computation.9 | async-start | bytes 8388608
  305.3 3.1 copy-start.10
  306.5 7.5 slice-start.3
  308.4 5.6 copy-start.11
  308.4 16.6 %slice-start = ((s8[8388608]{0:T(1024)(128)(4,1)}), s8[4194304]{0:T(1024)(128)(4,1)S(1)}, s32[]{:S(2)}) async-start(s8[8388608]{0:T(1024)(128)(4,1)} %bitcast.273), calls=%async_computation.7 | async-start | bytes 8388608
  314.0 11.0 slice-start.1
  328.8 1.2 copy-start.4
  328.8 2.0 copy-start
  329.1 0.9 copy-start.1
  599.8 1.8 copy-start.8
  1199.7 150.3 %all-to-all-start.1 = ((bf16[4,32,12288]{2,1,0:T(8,128)(2,1)}), bf16[4,32,12288]{2,1,0:T(8,128)(2,1)}, u32[]{:S(2)}, u32[]{:S(2)}) async-start(bf16[4,32,12288]{2,1,0:T(8,128)(2,1)} %bitcast.256), calls=%async_computation.1 | async-start | bytes 6291456 | tf_op jit(solution)/shard_map/all_to_all | solution.py:237
  1204.3 134.2 %all-reduce.21.cloned.1.call-start = ((), (), s32[]{:S(2)}) async-start(), calls=%async_computation.6 | async-start | bytes 147456
  1205.6 6.1 copy-start.2
Sparse Core Ops, SparseCore 0:
  10.9 70.7 all-gather.5
  84.6 54.3 all-gather.7
  141.9 77.3 all-gather.9
  222.0 76.1 all-gather.11
  1212.4 126.0 all-reduce.20
where the time goes:
time: 1370 us; the launch traced here: 1360 us
  blocking collectives  628 us (46%)
  matrix products  252 us (18%)
  waiting for transfers between devices  239 us (17%)
  local copies, waits for them, and re-layouts  175 us (13%)
  other arithmetic  46.6 us (3%)
  between operations  15.1 us (1%)
    all_to_all x1, blocking collectives, local(): lax.all_to_all(term.reshape(outer_count, D // outer_count, columns).astyp...  552 us
    unnamed x6, waiting for transfers between devices  123 us
    dynamic_update_slice x32, local copies, waits for them, and re-layouts, local(): lax.map(attend_back, (queries, keys_all, values_all, query_codes, d_heads...  106 us
    all_gather x1, waiting for transfers between devices, local(): lax.all_gather(down_weight, ('dp', 'fsdp'), axis=0, tiled=True)  66.6 us
    all_gather x1, waiting for transfers between devices, local(): lax.all_gather(up_weight, ('dp', 'fsdp'), axis=0, tiled=True)  49.5 us
    unnamed x1, blocking collectives  41.5 us
    dot_general x32, matrix products, scores_for(): jnp.einsum('dic,djc->dij', code_h, key_codes, preferred_element_type=f32)  37 us
    all_gather x1, blocking collectives, local(): lax.all_gather(up_bias, ('dp', 'fsdp'), axis=0, tiled=True)  34.3 us
  transfers between devices with their start and end apart: 6, of which 3 were waited for; matrix products, arithmetic and copies ran while one was open for 9% of the time, Pallas kernels for 0%

commit v1 on v0

--- a/solution.py
+++ b/solution.py
@@ -3,6 +3,7 @@
 import jax.numpy as jnp
 from jax import lax
 from jax.sharding import PartitionSpec as P
+from jax.lax import axis_index, axis_size, ppermute
 
 D = 1024
 H = 16
@@ -82,8 +83,25 @@
         lax.all_gather(first_shift, ("dp", "fsdp"), axis=0, tiled=True),
         lax.all_gather(rel_tables, ("dp", "fsdp"), axis=0, tiled=True),
     )
+
+    def drive_case(x_in, dim_at):
+        seen_now = axis_size(("dp", "fsdp"))
+        taken_in = axis_index(("dp", "fsdp"))
+        side_arr, then = (seen_now, taken_in)
+        finding, local_out = (x_in, 1)
+        while local_out < side_arr:
+            sides = []
+            for t in [*range(side_arr)]:
+                sides.append((t, t ^ local_out))
+            long_array = ppermute(finding, ("dp", "fsdp"), perm=sides)
+            mixed_arr = jnp.concatenate([finding, long_array], axis=dim_at)
+            h_now = jnp.concatenate([long_array, finding], axis=dim_at)
+            finding = jnp.where(then & local_out == 0, mixed_arr, h_now)
+            local_out = 2 * local_out
+        return finding
+
     up_full, down_full, upb_full, downb_full, gain_two, shift_two = (
-        lax.all_gather(up_weight, ("dp", "fsdp"), axis=0, tiled=True),
+        drive_case(up_weight, dim_at=0),
         lax.all_gather(down_weight, ("dp", "fsdp"), axis=0, tiled=True),
         lax.all_gather(up_bias, ("dp", "fsdp"), axis=0, tiled=True),
         lax.all_gather(down_bias, ("dp", "fsdp"), axis=0, tiled=True),

time: 1370 us -> 1530 us (1.12)
  waiting for transfers between devices: 239 us -> 322 us
  blocking collectives: 628 us -> 669 us
    ppermute x0 -> x5, waiting for transfers between devices: none -> 184 us  [drive_case(): long_array = ppermute(finding, ('dp', 'fsdp'), perm=sides)]
    all_gather x1, waiting for transfers between devices: 66.6 us -> 0.02 us  [local(): lax.all_gather(down_weight, ('dp', 'fsdp'), axis=0, tiled=True)]
    unnamed x1, blocking collectives: 41.5 us -> 82.5 us
    all_gather x1, waiting for transfers between devices: 49.5 us -> 16 us  [local(): lax.all_gather(up_weight, ('dp', 'fsdp'), axis=0, tiled=True)]
    unnamed x64 -> x96, local copies, waits for them, and re-layouts: 32.9 us -> 28.1 us
  transfers between devices with their start and end apart: 6 -> 11, of which waited for: 3 -> 6; matrix products, arithmetic and copies ran while one was open for 9% -> 11% of each run, Pallas kernels for 0% -> 0%
where the time goes in v1:
time: 1530 us; the launch traced here: 1520 us
  blocking collectives  669 us (44%)
  waiting for transfers between devices  322 us (21%)
  matrix products  255 us (17%)
  local copies, waits for them, and re-layouts  190 us (12%)
  other arithmetic  57.4 us (4%)
  between operations  15.3 us (1%)
    all_to_all x1, blocking collectives, local(): lax.all_to_all(term.reshape(outer_count, D // outer_count, columns).astyp...  552 us
    ppermute x5, waiting for transfers between devices, drive_case(): long_array = ppermute(finding, ('dp', 'fsdp'), perm=sides)  184 us
    unnamed x6, waiting for transfers between devices  122 us
    dynamic_update_slice x32, local copies, waits for them, and re-layouts, local(): lax.map(attend_back, (queries, keys_all, values_all, query_codes, d_heads...  106 us
    unnamed x1, blocking collectives  82.5 us
    dot_general x32, matrix products, scores_for(): jnp.einsum('dic,djc->dij', code_h, key_codes, preferred_element_type=f32)  37.1 us
    all_gather x1, blocking collectives, local(): lax.all_gather(up_bias, ('dp', 'fsdp'), axis=0, tiled=True)  34.1 us
  transfers between devices with their start and end apart: 11, of which 6 were waited for; matrix products, arithmetic and copies ran while one was open for 11% of the time, Pallas kernels for 0%

profile of v1, /device:TPU:8, one launch (start us, length us, event | category | flops | bytes accessed | tf_op | source)
XLA Modules:
  0.0 1519.0 jit_solution(12575823538123700840)
XLA Ops:
  14.1 13.8 collective-permute-done.1
  29.6 28.6 %collective-permute-done.2 = bf16[128,4096]{1,0:T(8,128)(2,1)} collective-permute-done((bf16[128,4096]{1,0:T(8,128)(2,1)S(1)}, bf16[128,4096]{1,0:T(8,128)(2,1)}, u32[]{:S(2)}, u32[]{:S(2)}) %collective-permute-start.2) | collective-permute-done | bytes 1048608 | tf_op jit(solution)/shard_map/ppermute | solution.py:96
  63.8 82.5 %all-reduce.18 = (bf16[2048]{0:T(1024)(128)(2,1)S(1)}, bf16[6144]{0:T(1024)(128)(2,1)S(1)}, bf16[1024]{0:T(1024)(128)(2,1)S(1)}, bf16[1024]{0:T(1024)(128)(2,1)S...) all-reduce(bf16[2048]{0:T(1024)(128)(2,1)S(1)} %dynamic-update-slic, ...), channel_id=1, replica_groups=mesh['dp'=8,'fsdp'=4] {'dp','fsdp'}, use_global_device_ids=true, to_apply=%add | all-reduce | flops 14336 | bytes 57344
  146.9 34.1 %all-gather = bf16[32,1,128]{2,1,0:T(2,128)(2,1)S(1)} all-gather(bf16[1,1,128]{2,1,0:T(2,128)(2,1)S(1)} %bitcast.273), channel_id=1, replica_groups=mesh['dp'=8,'fsdp'=4] {'dp','fsdp'}, dimensions={0}, use_global_device_ids=true | all-gather | bytes 8448 | tf_op jit(solution)/shard_map/all_gather | solution.py:106
  213.0 54.8 %while.31 = (s32[]{:T(128)}, bf16[16,1,169,64]{2,3,1,0:T(8,128)(2,1)S(1)}, f32[16,1,169]{2,1,0:T(1,128)}, pred[1,1,169]{2,1,0:T(4,128)(4,1)S(1)}, bf16[16,1,169,...) while((s32[]{:T(128)}, ...), condition=%wide.region_3.4_spmd.clone, body=%wide.region_0.3_spmd.clone.sunk | while | flops 29643952 | bytes 1992697 | solution.py:159
  271.0 140.2 %collective-permute-done.4 = bf16[512,4096]{1,0:T(8,128)(2,1)} collective-permute-done((bf16[512,4096]{1,0:T(8,128)(2,1)}, bf16[512,4096]{1,0:T(8,128)(2,1)}, u32[]{:S(2)}, u32[]{:S(2)}) %collective-permute-start.4) | collective-permute-done | bytes 4194336 | tf_op jit(solution)/shard_map/ppermute | solution.py:96
  411.3 14.7 multiply_convert_fusion.1
  426.1 7.0 fusion.131
  452.4 16.0 %all-gather.12.cloned.1.call-done = bf16[1024,4096]{1,0:T(8,128)(2,1)} async-done(((bf16[32,4096]{1,0:T(8,128)(2,1)}), bf16[1024,4096]{1,0:T(8,128)(2,1)}) %all-gather.12.cloned.1.call-update) | async-done | bytes 8388624 | tf_op jit(solution)/shard_map/all_gather | solution.py:180
  468.5 7.4 multiply_reduce_fusion.1
  482.3 272.6 %while.32 = (s32[]{:T(128)}, bf16[16,1,169,64]{2,3,1,0:T(8,128)(2,1)}, bf16[16,1,169,64]{2,3,1,0:T(8,128)(2,1)}, bf16[16,1,169,64]{2,3,1,0:T(8,128)(2,1)}, f32[1...) while((s32[]{:T(128)}, ...), condition=%wide.region_14.15_spmd.clone.clone, body=%wide.region_12.14_spmd.clone.clone.sunk | while | flops 162622784 | bytes 5006393 | solution.py:219
  492.8 6.5 dynamic_update_slice.47
  509.8 6.5 dynamic_update_slice.47
  526.8 6.5 dynamic_update_slice.47
  543.8 6.5 dynamic_update_slice.47
  560.8 6.5 dynamic_update_slice.47
  577.9 6.5 dynamic_update_slice.47
  594.9 6.5 dynamic_update_slice.47
  611.9 6.5 dynamic_update_slice.47
  628.9 6.5 dynamic_update_slice.47
  646.0 6.5 dynamic_update_slice.47
  663.0 6.5 dynamic_update_slice.47
  680.1 6.5 dynamic_update_slice.47
  697.2 6.5 dynamic_update_slice.47
  714.2 6.5 dynamic_update_slice.47
  731.3 6.5 dynamic_update_slice.47
  748.3 6.5 dynamic_update_slice.47
  763.7 8.7 copy.122
  772.3 17.5 %pad_maximum_fusion = bf16[1024,12288]{1,0:T(8,128)(2,1)} fusion(bf16[1024,4096]{1,0:T(8,128)(2,1)} %convolution_convert_fusion.2, bf16[1024,4096]{1,0:T(8,128)(2,1)} %convolution_convert_fusion.3, bf16[1024,1024]{1,0:T(8,128)(2,1)} %copy.123, bf16[1024,3072]{1,0:T(8,128)(2,1)} %copy.122), kind=kLoop, calls=%fused_computation.85 | loop fusion | flops 100663296 | bytes 50331648 | tf_op jit(solution)/shard_map/concatenate | solution.py:238
  789.9 552.2 %all_to_all.10 = bf16[8,128,12288]{2,1,0:T(8,128)(2,1)} all-to-all(bf16[8,128,12288]{2,1,0:T(8,128)(2,1)} %bitcast.251), channel_id=1, replica_groups=mesh['dp'=8,'fsdp'=4] {'dp'}, dimensions={0} | all-to-all | bytes 50331648 | tf_op jit(solution)/shard_map/all_to_all | solution.py:247
  1342.1 15.2 %reduce_sum.205 = bf16[128,12288]{1,0:T(8,128)(2,1)} reduce(bf16[8,128,12288]{2,1,0:T(8,128)(2,1)} %all_to_all.10, bf16[]{:T(256)} %constant.44.clone.1), dimensions={0}, to_apply=%region_15.16 | reduce | flops 11010048 | bytes 28311554 | tf_op jit(solution)/shard_map/reduce_sum | solution.py:254
  1376.1 119.7 %all-reduce.21.cloned.1.call-done = (f32[2048]{0:T(1024)}, f32[1024]{0:T(1024)}, f32[1024]{0:T(1024)}, f32[1024]{0:T(1024)}, f32[6144]{0:T(1024)}, /*index=5*/f3...) async-done(((f32[2048]{0:T(1024)}, f32[1024]{0:T(1024)}, f32[1024]{0:T(1024)}, f32[1024]{0:T(1024)}, f32[6144]{0:T(1024)}, /*index=5*/f32[4096]{0:T(1024)}, ...) | async-done | bytes 73744
  (601 shorter events, 340.5 us)
Async XLA Ops:
  7.2 195.2 %all-gather.6.cloned.1.call-start = ((), (), s32[]{:S(2)}) async-start(), calls=%async_computation.2 | async-start | bytes 6488064 | tf_op jit(solution)/shard_map/all_gather | solution.py:78
  7.9 259.9 %all-gather.8.cloned.1.call-start = ((), (), s32[]{:S(2)}) async-start(), calls=%async_computation.3 | async-start | bytes 2162688 | tf_op jit(solution)/shard_map/all_gather | solution.py:79
  8.7 417.4 %all-gather.10.cloned.1.call-start = ((), (), s32[]{:S(2)}) async-start(), calls=%async_computation.4 | async-start | bytes 8650752 | tf_op jit(solution)/shard_map/all_gather | solution.py:105
  9.4 459.1 %all-gather.12.cloned.1.call-start = ((), (), s32[]{:S(2)}) async-start(), calls=%async_computation.5 | async-start | bytes 8650752 | tf_op jit(solution)/shard_map/all_gather | solution.py:180
  9.4 1.8 collective-permute-start
  12.4 15.4 %collective-permute-start.1 = (bf16[64,4096]{1,0:T(8,128)(2,1)S(1)}, bf16[64,4096]{1,0:T(8,128)(2,1)S(1)}, u32[]{:S(2)}, u32[]{:S(2)}) collective-permute-start(bf16[64,4096]{1,0:T(8,128)(2,1)S(1)} %maximum_select_fusion.7), channel_id=1, source_target_pairs={{0,2},{1,3},{2,0},{3,1},{4,6},{5,7},{6,4},{7,5},{8,10},{9,11},{10,... | collective-permute-start | bytes 1572872 | tf_op jit(solution)/shard_map/ppermute | solution.py:96
  14.0 47.9 %copy-start.21 = (bf16[32]{0:T(256)(128)(2,1)S(1)}, bf16[32]{0:T(256)(128)(2,1)}, u32[]{:S(2)}) copy-start(bf16[32]{0:T(256)(128)(2,1)} %param.41) | copy-start | bytes 196
  14.0 48.1 %copy-start.22 = (bf16[32]{0:T(256)(128)(2,1)S(1)}, bf16[32]{0:T(256)(128)(2,1)}, u32[]{:S(2)}) copy-start(bf16[32]{0:T(256)(128)(2,1)} %param.39) | copy-start | bytes 196
  14.0 48.4 %copy-start.23 = (bf16[32]{0:T(256)(128)(2,1)S(1)}, bf16[32]{0:T(256)(128)(2,1)}, u32[]{:S(2)}) copy-start(bf16[32]{0:T(256)(128)(2,1)} %param.33) | copy-start | bytes 196
  14.0 48.6 %copy-start.24 = (bf16[32]{0:T(256)(128)(2,1)S(1)}, bf16[32]{0:T(256)(128)(2,1)}, u32[]{:S(2)}) copy-start(bf16[32]{0:T(256)(128)(2,1)} %param.34) | copy-start | bytes 196
  14.0 48.8 %copy-start.25 = (bf16[32]{0:T(256)(128)(2,1)S(1)}, bf16[32]{0:T(256)(128)(2,1)}, u32[]{:S(2)}) copy-start(bf16[32]{0:T(256)(128)(2,1)} %param.32) | copy-start | bytes 196
  14.0 49.0 %copy-start.26 = (bf16[32]{0:T(256)(128)(2,1)S(1)}, bf16[32]{0:T(256)(128)(2,1)}, u32[]{:S(2)}) copy-start(bf16[32]{0:T(256)(128)(2,1)} %param.40) | copy-start | bytes 196
  14.0 49.3 %copy-start.27 = (bf16[64]{0:T(256)(128)(2,1)S(1)}, bf16[64]{0:T(256)(128)(2,1)}, u32[]{:S(2)}) copy-start(bf16[64]{0:T(256)(128)(2,1)} %param.30) | copy-start | bytes 388
  14.0 49.5 %copy-start.28 = (bf16[192]{0:T(256)(128)(2,1)S(1)}, bf16[192]{0:T(256)(128)(2,1)}, u32[]{:S(2)}) copy-start(bf16[192]{0:T(256)(128)(2,1)} %param.35) | copy-start | bytes 1156
  14.0 132.9 %copy-start.20 = (bf16[128]{0:T(256)(128)(2,1)S(1)}, bf16[128]{0:T(256)(128)(2,1)}, u32[]{:S(2)}) copy-start(bf16[128]{0:T(256)(128)(2,1)} %param.37) | copy-start | bytes 772
  14.1 167.6 %copy-start.18 = (s32[1,169]{1,0:T(1,128)S(1)}, s32[1,169]{1,0:T(1,128)}, u32[]{:S(2)}) copy-start(s32[1,169]{1,0:T(1,128)} %param.27) | copy-start | bytes 2032
  14.1 167.6 %copy-start.19 = (s32[1,169]{1,0:T(1,128)S(1)}, s32[1,169]{1,0:T(1,128)}, u32[]{:S(2)}) copy-start(s32[1,169]{1,0:T(1,128)} %param.26) | copy-start | bytes 2032
  28.0 30.2 %collective-permute-start.2 = (bf16[128,4096]{1,0:T(8,128)(2,1)S(1)}, bf16[128,4096]{1,0:T(8,128)(2,1)}, u32[]{:S(2)}, u32[]{:S(2)}) collective-permute-start(bf16[128,4096]{1,0:T(8,128)(2,1)S(1)} %maximum_select_fusion.6), channel_id=1, source_target_pairs={{0,4},{1,5},{2,6},{3,7},{4,0},{5,1},{6,2},{7,3},{8,12},{9,13},{10,... | collective-permute-start | bytes 3145736 | tf_op jit(solution)/shard_map/ppermute | solution.py:96
  60.5 136.3 %collective-permute-start.3 = (bf16[256,4096]{1,0:T(8,128)(2,1)S(1)}, bf16[256,4096]{1,0:T(8,128)(2,1)}, u32[]{:S(2)}, u32[]{:S(2)}) collective-permute-start(bf16[256,4096]{1,0:T(8,128)(2,1)S(1)} %maximum_select_fusion.5), channel_id=1, source_target_pairs={{0,8},{1,9},{2,10},{3,11},{4,12},{5,13},{6,14},{7,15},{8,0},{9,1},... | collective-permute-start | bytes 6291464 | tf_op jit(solution)/shard_map/ppermute | solution.py:96
  201.7 209.6 %collective-permute-start.4 = (bf16[512,4096]{1,0:T(8,128)(2,1)}, bf16[512,4096]{1,0:T(8,128)(2,1)}, u32[]{:S(2)}, u32[]{:S(2)}) collective-permute-start(bf16[512,4096]{1,0:T(8,128)(2,1)} %maximum_select_fusion.4), channel_id=1, source_target_pairs={{0,16},{1,17},{2,18},{3,19},{4,20},{5,21},{6,22},{7,23},{8,24},{9,... | collective-permute-start | bytes 12582920 | tf_op jit(solution)/shard_map/ppermute | solution.py:96
  267.8 158.3 %copy-start.3 = (bf16[16,1,169,64]{2,3,1,0:T(8,128)(2,1)}, bf16[16,1,169,64]{2,3,1,0:T(8,128)(2,1)S(1)}, u32[]{:S(2)}) copy-start(bf16[16,1,169,64]{2,3,1,0:T(8,128)(2,1)S(1)} %get-tuple-element.138) | copy-start | bytes 1038340
  267.8 158.3 %copy-start.7 = (bf16[16,1,169,64]{3,2,1,0:T(8,128)(2,1)}, bf16[16,1,169,64]{3,2,1,0:T(8,128)(2,1)S(1)}, u32[]{:S(2)}) copy-start(bf16[16,1,169,64]{3,2,1,0:T(8,128)(2,1)S(1)} %get-tuple-element.785) | copy-start | bytes 1038340
  267.8 158.3 %copy-start.8 = (bf16[16,1,169,64]{3,2,1,0:T(8,128)(2,1)}, bf16[16,1,169,64]{3,2,1,0:T(8,128)(2,1)S(1)}, u32[]{:S(2)}) copy-start(bf16[16,1,169,64]{3,2,1,0:T(8,128)(2,1)S(1)} %get-tuple-element.786) | copy-start | bytes 1038340
  267.8 143.5 %copy-start.15 = (f32[32,1,128]{2,1,0:T(1,128)S(1)}, f32[32,1,128]{2,1,0:T(1,128)}, u32[]{:S(2)}) copy-start(f32[32,1,128]{2,1,0:T(1,128)} %convert_element_type.215) | copy-start | bytes 49156
  411.3 14.8 copy-start.17
  426.1 7.3 copy-start.11
  426.1 7.3 copy-start.16
  434.4 7.7 slice-start
  1357.4 6.0 copy-start.14
  1357.4 149.8 %all-to-all-start.1 = ((bf16[4,32,12288]{2,1,0:T(8,128)(2,1)}), bf16[4,32,12288]{2,1,0:T(8,128)(2,1)}, u32[]{:S(2)}, u32[]{:S(2)}) async-start(bf16[4,32,12288]{2,1,0:T(8,128)(2,1)} %bitcast.257), calls=%async_computation.1 | async-start | bytes 6291456 | tf_op jit(solution)/shard_map/all_to_all | solution.py:255
  1362.1 133.6 %all-reduce.21.cloned.1.call-start = ((), (), s32[]{:S(2)}) async-start(), calls=%async_computation.6 | async-start | bytes 147456
  1363.4 6.1 copy-start.2
  (11 other events, 36.0 us)
Sparse Core Ops, SparseCore 0:
  10.9 89.5 all-gather.5
  103.3 56.2 all-gather.7
  162.6 170.5 all-gather.9
  335.9 132.5 all-gather.11
  1369.7 126.0 all-reduce.20
